TPU v7x, 32 devices: a whole 2x2x4 slice. The times are simulated.
32 devices in a mesh: blocks: 8 (over z, core), lev: 4 (over y, x).
Axes of the slice: x: 2, y: 2, z: 4, core: 2. Of those that a mesh axis runs over, the one named last changes fastest.
Arguments:
- tracers: float32 [8, 4, 8, 128, 128], P('blocks', 'lev'), may hold values from -6 to 6
- east_velocity: float32 [8, 8, 128, 128], P('blocks'), may hold values from -0.24 to 0.24
- north_velocity: float32 [8, 8, 128, 128], P('blocks'), may hold values from -0.24 to 0.24
- upward_velocity: float32 [8, 8, 128, 128], P('blocks'), may hold values from -0.24 to 0.24
- target: float32 [8, 4, 8, 128, 128], P('blocks', 'lev'), may hold values from 0.09375 to 12.65625
- bottom: int32 [8, 128, 128], P('blocks'), may hold values from 0 to 8, as said below
- shave_fraction: float32 [8, 128, 128], P('blocks'), may hold values from 0.05 to 1, as said below
- side_bottom: int32 [8, 4, 128], P('blocks'), may hold values from 0 to 8, as said below
- neighbors: int32 [8, 4], P('blocks'), may hold values from -1 to 7, as said below
- fold_partner: int32 [8], P('blocks'), may hold values from -1 to 7, as said below
- thin_pairs: int32 [8, 2, 128], P('blocks'), may hold values from 0 to 16383, as said below
Outputs:
- new_tracers: float32 [8, 4, 8, 128, 128], P('blocks', 'lev')
Inputs may be any that keep to these rules, and one draw needn't show every extreme that they name: The blocks form a grid of 3 block columns, periodic from west to east, and 4 block rows; entries are mutual: neighbors[b,0] = c exactly when neighbors[c,1] = b, and neighbors[b,2] = c exactly when neighbors[c,3] = b; a block's entries that are not -1 differ; blocks of the top row have -1 to the north. `fold_partner`: set exactly for the blocks of the top row; mutual, a block may be its own partner. `bottom`: every block has wet columns. `side_bottom`: equals the bottom of the adjacent column or row of the neighbouring block, across the north fold the partner's top row in reversed order, 0 where no block lies. `thin_pairs`: thin cells of a block are distinct and have bottom 1 or more; each partner is the cell just east of its thin cell in the same row, with a bottom no smaller; no cell appears twice in a block. `shave_fraction`: listed thin cells have 0.05 to 0.2, all other cells 0.5 to 1.
All inputs are finite; a program needn't handle non-finite values.
Results may differ from a plain program's by a relative error of at most 0.0003.
Values sent between devices are 32-bit elements; how exact they have to be, the bound alone decides.
A program may use at most 64 MiB of HBM per device.

v0:
```python
import jax
import jax.numpy as jnp
from jax import lax
from jax.sharding import PartitionSpec as P

RATE = 0.5
facing_order = (1, 0, 3, 2)


def upwind(face, first, second):
    return jnp.maximum(face, 0.0) * first + jnp.minimum(face, 0.0) * second


def column_masks(levels, bottom, shave_fraction):
    level_grid = levels[None, None, :, None, None]
    column_bottom = bottom[:, None, None]
    wet = level_grid < column_bottom
    thick = jnp.where(
        level_grid < column_bottom - 1,
        1.0,
        jnp.where(level_grid == column_bottom - 1, shave_fraction[:, None, None], 0.0),
    )
    return (wet, thick)


def level_pair(field):
    zero_level = jnp.zeros_like(field[:, :, :1])
    return (
        jnp.concatenate([zero_level, field[:, :, :-1]], 2),
        jnp.concatenate([field[:, :, 1:], zero_level], 2),
    )


def advected_field(
    tracers,
    east_flow,
    north_flow,
    upward_flow,
    levels,
    bottom,
    wet,
    thick,
    side_bottom,
    west_pair,
    east_pair,
    south_pair,
    north_pair,
):
    level_grid = levels[None, None, :, None, None]
    column_bottom = bottom[:, None, None]
    edge_levels = levels[None, None, :, None]
    wet_west = edge_levels < side_bottom[:, 0][:, None, None, :]
    wet_east = edge_levels < side_bottom[:, 1][:, None, None, :]
    wet_south = edge_levels < side_bottom[:, 2][:, None, None, :]
    wet_north = edge_levels < side_bottom[:, 3][:, None, None, :]
    east_values = jnp.concatenate([tracers[..., 1:], east_pair[0][..., None]], -1)
    east_flows = jnp.concatenate([east_flow[..., 1:], east_pair[1][..., None]], -1)
    east_wets = jnp.concatenate([wet[..., 1:], wet_east[..., None]], -1)
    flux_east = upwind(
        jnp.where(wet & east_wets, 0.5 * (east_flow + east_flows), 0.0), tracers, east_values
    )
    west_face = jnp.where(wet_west & wet[..., 0], 0.5 * (west_pair[1] + east_flow[..., 0]), 0.0)
    flux_west = jnp.concatenate(
        [upwind(west_face, west_pair[0], tracers[..., 0])[..., None], flux_east[..., :-1]], -1
    )
    north_values = jnp.concatenate([tracers[..., 1:, :], north_pair[0][..., None, :]], -2)
    north_flows = jnp.concatenate([north_flow[..., 1:, :], north_pair[1][..., None, :]], -2)
    north_wets = jnp.concatenate([wet[..., 1:, :], wet_north[..., None, :]], -2)
    flux_north = upwind(
        jnp.where(wet & north_wets, 0.5 * (north_flow + north_flows), 0.0), tracers, north_values
    )
    south_face = jnp.where(
        wet_south & wet[..., 0, :], 0.5 * (south_pair[1] + north_flow[..., 0, :]), 0.0
    )
    flux_south = jnp.concatenate(
        [
            upwind(south_face, south_pair[0], tracers[..., 0, :])[..., None, :],
            flux_north[..., :-1, :],
        ],
        -2,
    )
    above_values, below_values = level_pair(tracers)
    above_flow, below_flow = level_pair(upward_flow)
    wet_above = (level_grid >= 1) & (level_grid - 1 < column_bottom)
    wet_below = level_grid + 1 < column_bottom
    flux_lower = upwind(
        jnp.where(wet & wet_below, 0.5 * (upward_flow + below_flow), 0.0), below_values, tracers
    )
    flux_upper = upwind(
        jnp.where(wet & wet_above, 0.5 * (above_flow + upward_flow), 0.0), tracers, above_values
    )
    divergence = flux_west - flux_east + flux_south - flux_north + flux_lower - flux_upper
    return tracers + jnp.where(wet, divergence / jnp.where(wet, thick, 1.0), 0.0)


def merge_block(field, bottom, shave_fraction, pairs, levels):
    flat = field.reshape(field.shape[0], field.shape[1], -1)
    thin_cells = pairs[0]
    partner = pairs[1]
    depth_index = bottom[thin_cells] - 1
    thin_thick = shave_fraction[thin_cells]
    partner_thick = jnp.where(bottom[partner] - 1 == depth_index, shave_fraction[partner], 1.0)
    thin_values = flat[:, :, thin_cells]
    partner_values = flat[:, :, partner]
    merged = (thin_thick * thin_values + partner_thick * partner_values) / (
        thin_thick + partner_thick
    )
    struck = levels[:, None] == depth_index[None, :]
    flat = flat.at[:, :, thin_cells].set(jnp.where(struck, merged, thin_values))
    flat = flat.at[:, :, partner].set(jnp.where(struck, merged, partner_values))
    return flat.reshape(field.shape)


def local(
    tracers,
    east_velocity,
    north_velocity,
    upward_velocity,
    target,
    bottom,
    shave_fraction,
    side_bottom,
    neighbors,
    fold_partner,
    thin_pairs,
):
    blocks_here, tracer_count, level_count, cells_side, _ = tracers.shape
    levels = jnp.arange(level_count, dtype=jnp.int32)
    east_flow = east_velocity[:, None]
    north_flow = north_velocity[:, None]
    upward_flow = upward_velocity[:, None]
    wet, thick = column_masks(levels, bottom, shave_fraction)
    restoring = RATE * (target - tracers)
    tracer_edges = jnp.stack(
        [
            tracers[..., 0],
            tracers[..., cells_side - 1],
            tracers[..., 0, :],
            tracers[..., cells_side - 1, :],
        ],
        1,
    )
    flow_edges = jnp.stack(
        [
            east_velocity[..., 0],
            east_velocity[..., cells_side - 1],
            north_velocity[..., 0, :],
            north_velocity[..., cells_side - 1, :],
        ],
        1,
    )
    tracer_piece = lax.all_gather(tracer_edges, "blocks", axis=0, tiled=True)
    flow_piece = lax.all_gather(flow_edges, "blocks", axis=0, tiled=True)
    owners = jnp.arange(tracer_piece.shape[0], dtype=jnp.int32)
    side_match = (neighbors[:, :, None] == owners[None, None, :]).astype(jnp.float32)
    fold_match = (fold_partner[:, None] == owners[None, :]).astype(jnp.float32)
    tracer_facing = jnp.stack([tracer_piece[:, side] for side in facing_order], 1)
    flow_facing = jnp.stack([flow_piece[:, side] for side in facing_order], 1)
    highest = lax.Precision.HIGHEST
    tracer_sides = jnp.einsum("bsq,qstlc->bstlc", side_match, tracer_facing, precision=highest)
    flow_sides = jnp.einsum("bsq,qslc->bslc", side_match, flow_facing, precision=highest)
    tracer_fold = jnp.einsum("bq,qtlc->btlc", fold_match, tracer_piece[:, 3], precision=highest)
    flow_fold = jnp.einsum("bq,qlc->blc", fold_match, flow_piece[:, 3], precision=highest)
    tracer_sides, flow_sides, tracer_fold, flow_fold = (
        tracer_sides,
        flow_sides,
        tracer_fold,
        flow_fold,
    )
    west_pair = (tracer_sides[:, 0], flow_sides[:, 0][:, None])
    east_pair = (tracer_sides[:, 1], flow_sides[:, 1][:, None])
    south_pair = (tracer_sides[:, 2], flow_sides[:, 2][:, None])
    north_pair = (
        tracer_sides[:, 3] + tracer_fold[..., ::-1],
        (flow_sides[:, 3] - flow_fold[..., ::-1])[:, None],
    )
    advected = advected_field(
        tracers,
        east_flow,
        north_flow,
        upward_flow,
        levels,
        bottom,
        wet,
        thick,
        side_bottom,
        west_pair,
        east_pair,
        south_pair,
        north_pair,
    )
    source_part = jnp.sum(jnp.where(wet, thick * restoring, 0.0))
    volume_part = tracer_count * jnp.sum(jnp.where(wet, thick, 0.0))
    total_source, total_volume = lax.psum((source_part, volume_part), ("blocks", "lev"))
    stepped = jnp.where(wet, advected + restoring - total_source / total_volume, 0.0)
    return jax.vmap(merge_block, in_axes=(0, 0, 0, 0, None))(
        stepped,
        bottom.reshape(blocks_here, -1),
        shave_fraction.reshape(blocks_here, -1),
        thin_pairs,
        levels,
    )


def solution(mesh):
    placed = (
        P("blocks", "lev", None, None, None),
        P("blocks", None, None, None),
        P("blocks", None, None, None),
        P("blocks", None, None, None),
        P("blocks", "lev", None, None, None),
        P("blocks", None, None),
        P("blocks", None, None),
        P("blocks", None, None),
        P("blocks", None),
        P("blocks"),
        P("blocks", None, None),
    )
    return jax.shard_map(
        local,
        mesh=mesh,
        in_specs=placed,
        out_specs=P("blocks", "lev", None, None, None),
        check_vma=False,
    )
```

profile of v0, /device:TPU:0, one launch (start us, length us, event | category | flops | bytes accessed | tf_op | source)
XLA Modules:
  0.0 142.8 jit_solution(14295205948113703087)
XLA Ops:
  2.0 0.8 compare_select_fusion
  3.4 1.8 %gather_fusion.4 = f32[128]{0:T(128)S(1)} fusion(f32[1,16384]{1,0:T(1,128)} %bitcast.215, s32[128]{0:T(128)S(1)} %get-tuple-element.43), kind=kCustom, calls=%fused_computation.4 | custom fusion | bytes 2048 | tf_op jit(solution)/shard_map/vmap()/gather | solution.py:102
  5.1 1.8 %gather_fusion.3 = s32[128]{0:T(128)S(1)} fusion(s32[1,16384]{1,0:T(1,128)} %bitcast.212, s32[128]{0:T(128)S(1)} %get-tuple-element.43), kind=kCustom, calls=%fused_computation.3 | custom fusion | bytes 2048 | tf_op jit(solution)/shard_map/vmap()/gather | solution.py:102
  7.5 1.8 %gather_fusion.1 = f32[128]{0:T(128)S(1)} fusion(f32[1,16384]{1,0:T(1,128)} %bitcast.216, s32[128]{0:T(128)S(1)} %get-tuple-element.46), kind=kCustom, calls=%fused_computation.1 | custom fusion | bytes 2048 | tf_op jit(solution)/shard_map/vmap()/gather | solution.py:101
  9.2 1.8 %gather_fusion = s32[128]{0:T(128)S(1)} fusion(s32[1,16384]{1,0:T(1,128)} %bitcast.213, s32[128]{0:T(128)S(1)} %get-tuple-element.46), kind=kCustom, calls=%fused_computation | custom fusion | bytes 2048 | tf_op jit(solution)/shard_map/vmap()/gather | solution.py:100
  11.6 1.4 slice_bitcast_fusion.15
  13.5 0.8 fusion.78
  14.3 0.8 fusion.77
  15.1 0.9 copy.208
  16.0 0.9 copy.235
  16.9 0.9 broadcast_add_fusion
  19.2 0.9 slice.230
  20.0 1.3 copy.236
  21.3 15.7 %all_gather.7 = f32[8,4,1,8,128]{4,3,2,1,0:T(8,128)S(1)} all-gather(f32[1,4,1,8,128]{4,3,2,1,0:T(8,128)S(1)} %pad_maximum_fusion.2), channel_id=1, replica_groups=mesh['blocks'=8,'lev'=4] {'blocks'}, dimensions={0}, use_global_device_ids=true | all-gather | bytes 147456 | tf_op jit(solution)/shard_map/all_gather | solution.py:152
  37.6 1.0 copy.227
  38.6 0.8 slice.223
  39.5 1.3 copy.209
  40.8 14.0 %all_gather.6 = f32[8,4,8,128]{3,2,1,0:T(8,128)S(1)} all-gather(f32[1,4,8,128]{3,2,1,0:T(8,128)S(1)} %pad_maximum_fusion.1), channel_id=1, replica_groups=mesh['blocks'=8,'lev'=4] {'blocks'}, dimensions={0}, use_global_device_ids=true | all-gather | bytes 147456 | tf_op jit(solution)/shard_map/all_gather | solution.py:153
  55.3 1.0 copy.224
  56.3 0.8 slice.221
  57.6 1.3 copy.221
  59.8 1.0 copy.228
  61.3 4.0 %select_reduce_fusion = (f32[]{:T(128)}, f32[]{:T(128)}, f32[1,1,8,128,128]{3,2,4,1,0:T(8,128)}, f32[1,1,8,128,128]{3,2,4,1,0:T(8,128)S(1)}) fusion(f32[128,128]{0,1:T(8,128)S(1)} %copy.235, s32[128,128]{0,1:T(8,128)S(1)} %copy.234, s32[128,128]{0,1:T(8,128)S(1)} %copy.208, f32[1,1,8,128,128]{3,2,4,1,0:T(8,128)S(1)} %copy.237, ...), kind=kLoop, calls=%fused_computation.28 | loop fusion | flops 4718590 | bytes 5701640 | tf_op jit(solution)/shard_map/reduce_sum | solution.py:193
  65.3 40.5 %all-reduce.4 = (f32[]{:T(128)}, f32[]{:T(128)}) all-reduce(f32[]{:T(128)} %get-tuple-element.6, f32[]{:T(128)} %get-tuple-element.5), channel_id=1, replica_groups=mesh['blocks'=8,'lev'=4] {'blocks','lev'}, use_global_device_ids=true, to_apply=%region_1.2 | all-reduce | flops 2 | bytes 16 | tf_op jit(solution)/shard_map/psum | solution.py:194
  107.1 1.1 slice.225
  108.3 2.3 %subtract_select_fusion = f32[1,1,8,128,128]{3,2,4,1,0:T(8,128)S(1)} fusion(f32[1,1,8,128,128]{3,2,4,1,0:T(8,128)S(1)} %copy.236, f32[1,1,8,128,128]{3,2,4,1,0:T(8,128)S(1)} %get-tuple-element.12, f32[1,1,8,127,128]{3,2,4,1,0:T(8,128)S(1)} %bitcast.223, f32[1,1,8,1,128]{3,2,4,1,0:T(8,128)} %copy.228, f32[1,1,8,128,128]{3,2,4,1,0:T(8,128)} %get-tuple-element.11, ...), kind=kLoop, calls=%fused_computation.27 | loop fusion | flops 5505024 | bytes 6225996 | tf_op jit(solution)/shard_map/jit(_where)/select_n | solution.py:195
  110.6 7.4 %copy.239 = f32[1,1,8,128,128]{2,4,3,1,0:T(8,128)} copy(f32[1,1,8,128,128]{3,2,4,1,0:T(8,128)S(1)} %subtract_select_fusion) | data formatting | bytes 1048576 | tf_op jit(solution)/shard_map/jit(_where)/select_n | solution.py:195
  118.0 1.8 %gather_fusion.5 = f32[128,8]{1,0:T(8,128)S(1)} fusion(f32[1,8,16384]{1,2,0:T(8,128)} %bitcast.208, s32[128]{0:T(128)S(1)} %get-tuple-element.43), kind=kCustom, calls=%fused_computation.5 | custom fusion | bytes 9216 | tf_op jit(solution)/shard_map/vmap()/gather | solution.py:104
  119.8 1.8 %gather_fusion.2 = f32[128,8]{1,0:T(8,128)S(1)} fusion(f32[1,8,16384]{1,2,0:T(8,128)} %bitcast.209, s32[128]{0:T(128)S(1)} %get-tuple-element.46), kind=kCustom, calls=%fused_computation.2 | custom fusion | bytes 9216 | tf_op jit(solution)/shard_map/vmap()/gather | solution.py:103
  121.6 7.7 %scatter_custom_fusion = f32[8,16384]{0,1:T(8,128)} fusion(f32[8,16384]{0,1:T(8,128)} %bitcast.210, s32[128]{0:T(128)} %get-tuple-element.47, f32[128,8]{1,0:T(8,128)S(1)} %gather_fusion.2, f32[128,8]{1,0:T(8,128)S(1)} %gather_fusion.5, f32[128]{0:T(128)S(1)} %gather_fusion.1, s32[128]{0:T(128)S(1)} %broadcast_add_fusion.1, f32[128]{0:T(128)S(1)} %get-tuple-element.9, ...), kind=kCustom, calls=%fused_computation.47 | custom fusion | flops 6144 | bytes 534528 | tf_op jit(solution)/shard_map/vmap()/scatter | solution.py:109
  129.3 7.7 %scatter_custom_fusion.1 = f32[8,16384]{0,1:T(8,128)} fusion(f32[8,16384]{0,1:T(8,128)} %scatter_custom_fusion, s32[128]{0:T(128)} %get-tuple-element.42, f32[128,8]{1,0:T(8,128)S(1)} %gather_fusion.5, f32[128,8]{1,0:T(8,128)S(1)} %gather_fusion.2, f32[128]{0:T(128)S(1)} %gather_fusion.1, s32[128]{0:T(128)S(1)} %broadcast_add_fusion.1, ...), kind=kCustom, calls=%fused_computation.45 | custom fusion | flops 6144 | bytes 534528 | tf_op jit(solution)/shard_map/vmap()/scatter | solution.py:110
  136.9 5.9 %copy.241 = f32[1,1,8,128,128]{4,3,2,1,0:T(8,128)} copy(f32[1,1,8,128,128]{2,4,3,1,0:T(8,128)} %bitcast.211) | data formatting | bytes 1048576 | tf_op jit(solution)/shard_map/vmap()/reshape | solution.py:111
  (43 shorter events, 7.8 us)
Async XLA Ops:
  0.0 57.4 %copy-start.1 = (f32[1,1,8,128,128]{4,3,2,1,0:T(8,128)S(1)}, f32[1,1,8,128,128]{4,3,2,1,0:T(8,128)}, u32[]{:S(2)}) copy-start(f32[1,1,8,128,128]{4,3,2,1,0:T(8,128)} %param.15) | copy-start | bytes 1572868
  0.0 57.2 %copy-start = (f32[1,8,128,128]{3,2,1,0:T(8,128)S(1)}, f32[1,8,128,128]{3,2,1,0:T(8,128)}, u32[]{:S(2)}) copy-start(f32[1,8,128,128]{3,2,1,0:T(8,128)} %param.14) | copy-start | bytes 1572868
where the time goes:
time: 144 us; the launch traced here: 143 us
  blocking collectives  70.2 us (49%)
  local copies, waits for them, and re-layouts  41.9 us (29%)
  other arithmetic  27.6 us (19%)
  between operations  2.28 us (2%)
    psum x1, blocking collectives, local(): lax.psum((source_part, volume_part), ('blocks', 'lev'))  40.5 us
    all_gather x1, blocking collectives, local(): tracer_piece = lax.all_gather(tracer_edges, 'blocks', axis=0, tiled=True)  15.7 us
    all_gather x1, blocking collectives, local(): flow_piece = lax.all_gather(flow_edges, 'blocks', axis=0, tiled=True)  14 us
    scatter x2, other arithmetic, merge_block(): flat = flat.at[:, :, thin_cells].set(jnp.where(struck, merged, thin_values))  8.27 us
    scatter x1, other arithmetic, merge_block(): flat = flat.at[:, :, partner].set(jnp.where(struck, merged, partner_values))  7.68 us
    select_n x1, local copies, waits for them, and re-layouts, local(): jnp.where(wet, advected + restoring - total_source / total_volume, 0.0)  7.4 us
    reshape x1, local copies, waits for them, and re-layouts, merge_block(): return flat.reshape(field.shape)  5.85 us
    unnamed x9, local copies, waits for them, and re-layouts  4.29 us

commit v1 on v0

--- a/solution.py
+++ b/solution.py
@@ -1,10 +1,41 @@
+import functools
 import jax
 import jax.numpy as jnp
 from jax import lax
 from jax.sharding import PartitionSpec as P
+from jax.lax import axis_index, ppermute, psum
 
 RATE = 0.5
 facing_order = (1, 0, 3, 2)
+
+
+def plan_page_on(slab_in, chip_axis):
+    t1 = psum(1, chip_axis)
+    state_next = axis_index(chip_axis)
+    res, frame_out, extra = (t1, state_next, slab_in.shape[0])
+    oldest = range(res)
+    x_next = range(res)
+    copies = list(map(lambda t: (t, (t + 1) % res), oldest))
+    earlier = map(lambda t: (t, (t - 1) % res), x_next)
+    piece_out = jnp.zeros((*slab_in.shape[:0], res * extra, *slab_in.shape[1:]), slab_in.dtype)
+    piece_out = lax.dynamic_update_slice_in_dim(piece_out, slab_in, frame_out * extra, axis=0)
+    current_arr = a_now = slab_in
+    prior = res // 2
+    windows = list(earlier)
+    for u in range(1, prior + 1):
+        current_arr = ppermute(current_arr, chip_axis, copies)
+        piece_out = lax.dynamic_update_slice_in_dim(
+            piece_out, current_arr, (frame_out - u) % res * extra, axis=0
+        )
+        if u < res - prior:
+            a_now = ppermute(a_now, chip_axis, perm=windows)
+            piece_out = lax.dynamic_update_slice_in_dim(
+                piece_out, a_now, (frame_out + u) % res * extra, axis=0
+            )
+    return piece_out
+
+
+_find_tasks = functools.partial(plan_page_on, chip_axis="blocks")
 
 
 def upwind(face, first, second):
@@ -149,7 +180,7 @@
         ],
         1,
     )
-    tracer_piece = lax.all_gather(tracer_edges, "blocks", axis=0, tiled=True)
+    tracer_piece = _find_tasks(tracer_edges)
     flow_piece = lax.all_gather(flow_edges, "blocks", axis=0, tiled=True)
     owners = jnp.arange(tracer_piece.shape[0], dtype=jnp.int32)
     side_match = (neighbors[:, :, None] == owners[None, None, :]).astype(jnp.float32)

time: 144 us -> 155 us (1.076)
  blocking collectives: 70.2 us -> 52.5 us
  starting transfers between devices: 0 us -> 11.6 us
  other arithmetic: 27.6 us -> 35 us
  local copies, waits for them, and re-layouts: 41.9 us -> 46.6 us
  waiting for transfers between devices: 0 us -> 3.98 us
    all_gather x1 -> x0, blocking collectives: 15.7 us -> none  [local(): tracer_piece = lax.all_gather(tracer_edges, 'blocks', axis=0, tiled=True)]
    ppermute x0 -> x7, starting transfers between devices: none -> 11.6 us  [the longest x3 10.8 us: plan_page_on(): a_now = ppermute(a_now, chip_axis, perm=windows)]
    dynamic_update_slice x0 -> x7, local copies, waits for them, and re-layouts: none -> 5.63 us  [the longest x4 3.11 us: plan_page_on(): lax.dynamic_update_slice_in_dim(piece_out, current_arr, (frame_out - u) %...]
    add x0 -> x4, other arithmetic: none -> 4.35 us  [the longest x1 2.19 us: advected_field(): north_flow + north_flows]
    ppermute x0 -> x7, waiting for transfers between devices: none -> 3.98 us  [the longest x4 3.97 us: plan_page_on(): current_arr = ppermute(current_arr, chip_axis, copies)]
    select_n x1, local copies, waits for them, and re-layouts: 7.4 us -> 4.63 us  [local(): jnp.where(wet, advected + restoring - total_source / total_volume, 0.0)]
    slice x1, local copies, waits for them, and re-layouts: 0.14 us -> 2.74 us  [level_pair(): field[:, :, 1:]]
    concatenate x2 -> x0, local copies, waits for them, and re-layouts: 2.07 us -> none  [the longest x1 1.04 us: advected_field(): jnp.concatenate([north_flow[..., 1:, :], north_pair[1][..., None, :]], -2)]
  transfers between devices with their start and end apart: 0 -> 7, of which waited for: 0 -> 2; matrix products, arithmetic and copies ran while one was open for 0% -> 26% of each run, Pallas kernels for 0% -> 0%
where the time goes in v1:
time: 155 us; the launch traced here: 153 us
  blocking collectives  52.5 us (34%)
  local copies, waits for them, and re-layouts  46.6 us (30%)
  other arithmetic  35 us (23%)
  starting transfers between devices  11.6 us (7%)
  waiting for transfers between devices  3.98 us (3%)
  between operations  2.33 us (2%)
    psum x1, blocking collectives, local(): lax.psum((source_part, volume_part), ('blocks', 'lev'))  38.6 us
    all_gather x1, blocking collectives, local(): flow_piece = lax.all_gather(flow_edges, 'blocks', axis=0, tiled=True)  14 us
    ppermute x3, starting transfers between devices, plan_page_on(): a_now = ppermute(a_now, chip_axis, perm=windows)  10.8 us
    scatter x2, other arithmetic, merge_block(): flat = flat.at[:, :, thin_cells].set(jnp.where(struck, merged, thin_values))  8.27 us
    scatter x1, other arithmetic, merge_block(): flat = flat.at[:, :, partner].set(jnp.where(struck, merged, partner_values))  7.73 us
    reshape x1, local copies, waits for them, and re-layouts, merge_block(): return flat.reshape(field.shape)  5.85 us
    select_n x1, local copies, waits for them, and re-layouts, local(): jnp.where(wet, advected + restoring - total_source / total_volume, 0.0)  4.63 us
    unnamed x33, local copies, waits for them, and re-layouts  4.54 us
  transfers between devices with their start and end apart: 7, of which 2 were waited for; matrix products, arithmetic and copies ran while one was open for 26% of the time, Pallas kernels for 0%

profile of v1, /device:TPU:0, one launch (start us, length us, event | category | flops | bytes accessed | tf_op | source)
XLA Modules:
  0.0 152.9 jit_solution(7835337994728739838)
XLA Ops:
  0.0 0.9 fusion.73
  0.9 1.3 copy.69
  3.3 4.0 %collective-permute-start.1 = (f32[1,4,1,8,128]{4,3,2,1,0:T(8,128)}, f32[1,4,1,8,128]{4,3,2,1,0:T(8,128)}, u32[]{:S(2)}, u32[]{:S(2)}) collective-permute-start(f32[1,4,1,8,128]{4,3,2,1,0:T(8,128)} %get-tuple-element.39), channel_id=1, source_target_pairs={{0,28},{4,0},{8,4},{12,8},{16,12},{20,16},{24,20},{28,24},{1,29},{... | collective-permute-start | bytes 49160 | tf_op jit(solution)/shard_map/ppermute | solution.py:31
  8.7 2.3 %gather_fusion.4 = f32[128]{0:T(128)} fusion(f32[1,16384]{1,0:T(1,128)} %bitcast.219, s32[128]{0:T(128)S(1)} %get-tuple-element.46), kind=kCustom, calls=%fused_computation.4 | custom fusion | bytes 2048 | tf_op jit(solution)/shard_map/vmap()/gather | solution.py:133
  11.0 2.3 %gather_fusion.3 = s32[128]{0:T(128)} fusion(s32[1,16384]{1,0:T(1,128)} %bitcast.214, s32[128]{0:T(128)S(1)} %get-tuple-element.46), kind=kCustom, calls=%fused_computation.3 | custom fusion | bytes 2048 | tf_op jit(solution)/shard_map/vmap()/gather | solution.py:133
  13.8 2.4 %gather_fusion.1 = f32[128]{0:T(128)} fusion(f32[1,16384]{1,0:T(1,128)} %bitcast.220, s32[128]{0:T(128)S(1)} %get-tuple-element.49), kind=kCustom, calls=%fused_computation.1 | custom fusion | bytes 2048 | tf_op jit(solution)/shard_map/vmap()/gather | solution.py:132
  16.2 1.8 %gather_fusion = s32[128]{0:T(128)S(1)} fusion(s32[1,16384]{1,0:T(1,128)} %bitcast.215, s32[128]{0:T(128)S(1)} %get-tuple-element.49), kind=kCustom, calls=%fused_computation | custom fusion | bytes 2048 | tf_op jit(solution)/shard_map/vmap()/gather | solution.py:131
  18.5 1.5 broadcast_add_fusion
  21.8 1.4 slice_bitcast_fusion.16
  24.4 0.9 iota_compare_fusion.2
  25.3 1.3 copy.64
  26.6 1.4 copy.131
  27.9 14.0 %all_gather.3 = f32[8,4,8,128]{3,2,1,0:T(8,128)S(1)} all-gather(f32[1,4,8,128]{3,2,1,0:T(8,128)S(1)} %pad_maximum_fusion.1), channel_id=1, replica_groups=mesh['blocks'=8,'lev'=4] {'blocks'}, dimensions={0}, use_global_device_ids=true | all-gather | bytes 147456 | tf_op jit(solution)/shard_map/all_gather | solution.py:184
  43.6 2.7 %fusion.71 = (f32[1,1,7,128,128]{4,3,2,1,0:T(8,128)}, f32[1,1,7,128,128]{4,3,2,1,0:T(8,128)}, f32[1,1,7,128,128]{4,3,2,1,0:T(8,128)}, f32[1,1,7,128,128]{4,3,2,1,0:T(8,128)}) fusion(f32[1,1,8,128,128]{4,3,2,1,0:T(8,128)} %bitcast.226, f32[1,1,8,128,128]{4,3,2,1,0:T(8,128)} %param.11), kind=kLoop, calls=%fused_computation.153 | loop fusion | bytes 3670016 | tf_op jit(solution)/shard_map/slice | solution.py:61
  47.8 2.2 %maximum_add_fusion.1 = f32[1,1,8,128,128]{4,2,3,1,0:T(8,128)} fusion(f32[1,1,8,1,128]{4,2,3,1,0:T(8,128)S(1)} %fusion.43, f32[1,1,8,127,128]{4,2,3,1,0:T(8,128)} %slice.233, f32[1,8,128,128]{3,2,1,0:T(8,128)S(1)} %copy-done.4), kind=kLoop, calls=%fused_computation.14 | loop fusion | flops 262144 | bytes 1572864 | tf_op jit(solution)/shard_map/add | solution.py:101
  50.0 1.3 fusion.70
  55.2 1.3 copy.83
  58.3 3.2 %collective-permute-start.3 = (f32[1,4,1,8,128]{4,3,2,1,0:T(8,128)}, f32[1,4,1,8,128]{4,3,2,1,0:T(8,128)S(1)}, u32[]{:S(2)}, u32[]{:S(2)}) collective-permute-start(f32[1,4,1,8,128]{4,3,2,1,0:T(8,128)} %collective-permute-done.1), channel_id=1, source_target_pairs={{0,28},{4,0},{8,4},{12,8},{16,12},{20,16},{24,20},{28,24},{1,29},{... | collective-permute-start | bytes 49160 | tf_op jit(solution)/shard_map/ppermute | solution.py:31
  61.5 1.3 constant_dynamic-update-slice_fusion.6
  62.8 1.3 constant_dynamic-update-slice_fusion.5
  64.1 3.5 %collective-permute-start.5 = (f32[1,4,1,8,128]{4,3,2,1,0:T(8,128)S(1)}, f32[1,4,1,8,128]{4,3,2,1,0:T(8,128)S(1)}, u32[]{:S(2)}, u32[]{:S(2)}) collective-permute-start(f32[1,4,1,8,128]{4,3,2,1,0:T(8,128)S(1)} %collective-permute-done.3), channel_id=1, source_target_pairs={{0,28},{4,0},{8,4},{12,8},{16,12},{20,16},{24,20},{28,24},{1,29},{... | collective-permute-start | bytes 49160 | tf_op jit(solution)/shard_map/ppermute | solution.py:31
  70.3 3.7 %collective-permute-done.6 = f32[1,4,1,8,128]{4,3,2,1,0:T(8,128)S(1)} collective-permute-done((f32[1,4,1,8,128]{4,3,2,1,0:T(8,128)S(1)}, f32[1,4,1,8,128]{4,3,2,1,0:T(8,128)S(1)}, u32[]{:S(2)}, u32[]{:S(2)}) %collective-permute-start.6) | collective-permute-done | bytes 16416 | tf_op jit(solution)/shard_map/ppermute | solution.py:26
  76.7 1.5 fusion.2
  78.6 2.3 %select_reduce_fusion = (f32[]{:T(128)}, f32[]{:T(128)}, f32[1,1,8,128,128]{4,3,2,1,0:T(8,128)S(1)}) fusion(f32[128,128]{1,0:T(8,128)S(1)} %bitcast.221, s32[128,128]{1,0:T(8,128)S(1)} %copy-done.6, s32[128,128]{1,0:T(8,128)S(1)} %bitcast.217, f32[1,1,8,128,128]{4,3,2,1,0:T(8,128)} %param.15, f32[1,1,8,128,128]{4,3,2,1,0:T(8,128)S(1)} %copy-done.2, ...), kind=kLoop, calls=%fused_computation.28 | loop fusion | flops 2883582 | bytes 2949128 | tf_op jit(solution)/shard_map/reduce_sum | solution.py:224
  80.9 38.6 %all-reduce.4 = (f32[]{:T(128)}, f32[]{:T(128)}) all-reduce(f32[]{:T(128)} %get-tuple-element.6, f32[]{:T(128)} %get-tuple-element.5), channel_id=1, replica_groups=mesh['blocks'=8,'lev'=4] {'blocks','lev'}, use_global_device_ids=true, to_apply=%region_1.2 | all-reduce | flops 2 | bytes 16 | tf_op jit(solution)/shard_map/psum | solution.py:225
  120.9 2.5 %subtract_select_fusion = f32[1,1,8,128,128]{4,3,2,1,0:T(8,128)S(1)} fusion(f32[1,1,8,128,128]{4,3,2,1,0:T(8,128)S(1)} %copy-done.2, f32[1,1,8,128,128]{4,3,2,1,0:T(8,128)S(1)} %get-tuple-element.11, f32[1,1,8,128,128]{4,3,2,1,0:T(8,128)S(1)} %copy.86, f32[1,1,8,127,128]{4,3,2,1,0:T(8,128)S(1)} %bitcast.225, f32[1,1,8,1,128]{4,3,2,1,0:T(1,128)S(1)} %bitcast.236, ...), kind=kLoop, calls=%fused_computation.27 | loop fusion | flops 5242880 | bytes 5701708 | tf_op jit(solution)/shard_map/jit(_where)/select_n | solution.py:226
  123.3 4.6 %copy.87 = f32[1,1,8,128,128]{2,4,3,1,0:T(8,128)} copy(f32[1,1,8,128,128]{4,3,2,1,0:T(8,128)S(1)} %subtract_select_fusion) | data formatting | bytes 1048576 | tf_op jit(solution)/shard_map/jit(_where)/select_n | solution.py:226
  128.0 1.8 %gather_fusion.5 = f32[128,8]{1,0:T(8,128)S(1)} fusion(f32[1,8,16384]{1,2,0:T(8,128)} %bitcast.210, s32[128]{0:T(128)S(1)} %get-tuple-element.46), kind=kCustom, calls=%fused_computation.5 | custom fusion | bytes 9216 | tf_op jit(solution)/shard_map/vmap()/gather | solution.py:135
  129.7 1.8 %gather_fusion.2 = f32[128,8]{1,0:T(8,128)S(1)} fusion(f32[1,8,16384]{1,2,0:T(8,128)} %bitcast.211, s32[128]{0:T(128)S(1)} %get-tuple-element.49), kind=kCustom, calls=%fused_computation.2 | custom fusion | bytes 9216 | tf_op jit(solution)/shard_map/vmap()/gather | solution.py:134
  131.6 7.7 %scatter_custom_fusion = f32[8,16384]{0,1:T(8,128)} fusion(f32[8,16384]{0,1:T(8,128)} %bitcast.212, s32[128]{0:T(128)} %get-tuple-element.50, f32[128,8]{1,0:T(8,128)S(1)} %gather_fusion.2, f32[128,8]{1,0:T(8,128)S(1)} %gather_fusion.5, f32[128]{0:T(128)S(1)} %copy-done.9, s32[128]{0:T(128)S(1)} %copy-done.12, f32[128]{0:T(128)S(1)} %copy-done.10, ...), kind=kCustom, calls=%fused_computation.47 | custom fusion | flops 6144 | bytes 534528 | tf_op jit(solution)/shard_map/vmap()/scatter | solution.py:140
  139.3 7.7 %scatter_custom_fusion.1 = f32[8,16384]{0,1:T(8,128)} fusion(f32[8,16384]{0,1:T(8,128)} %scatter_custom_fusion, s32[128]{0:T(128)} %get-tuple-element.45, f32[128,8]{1,0:T(8,128)S(1)} %gather_fusion.5, f32[128,8]{1,0:T(8,128)S(1)} %gather_fusion.2, f32[128]{0:T(128)S(1)} %copy-done.9, s32[128]{0:T(128)S(1)} %copy-done.12, f32[128]{0:T(128)S(1)} %copy-done.10, ...), kind=kCustom, calls=%fused_computation.45 | custom fusion | flops 6144 | bytes 534528 | tf_op jit(solution)/shard_map/vmap()/scatter | solution.py:141
  147.0 5.9 %copy.89 = f32[1,1,8,128,128]{4,3,2,1,0:T(8,128)} copy(f32[1,1,8,128,128]{2,4,3,1,0:T(8,128)} %bitcast.213) | data formatting | bytes 1048576 | tf_op jit(solution)/shard_map/vmap()/reshape | solution.py:142
  (86 shorter events, 20.4 us)
Async XLA Ops:
  0.0 54.3 %copy-start.2 = (f32[1,1,8,128,128]{4,3,2,1,0:T(8,128)S(1)}, f32[1,1,8,128,128]{4,3,2,1,0:T(8,128)}, u32[]{:S(2)}) copy-start(f32[1,1,8,128,128]{4,3,2,1,0:T(8,128)} %param.11) | copy-start | bytes 1572868
  0.0 47.8 %copy-start.4 = (f32[1,8,128,128]{3,2,1,0:T(8,128)S(1)}, f32[1,8,128,128]{3,2,1,0:T(8,128)}, u32[]{:S(2)}) copy-start(f32[1,8,128,128]{3,2,1,0:T(8,128)} %param.13) | copy-start | bytes 1572868
  2.8 10.5 %copy-start.7 = (f32[8,4,1,8,128]{4,3,2,1,0:T(8,128)}, f32[8,4,1,8,128]{4,3,2,1,0:T(8,128)S(1)}, u32[]{:S(2)}) copy-start(f32[8,4,1,8,128]{4,3,2,1,0:T(8,128)S(1)} %get-tuple-element.40) | copy-start | bytes 393220
  2.8 55.2 %collective-permute-start = (f32[1,4,1,8,128]{4,3,2,1,0:T(8,128)}, f32[1,4,1,8,128]{4,3,2,1,0:T(8,128)}, u32[]{:S(2)}, u32[]{:S(2)}) collective-permute-start(f32[1,4,1,8,128]{4,3,2,1,0:T(8,128)} %get-tuple-element.39), channel_id=1, source_target_pairs={{0,4},{4,8},{8,12},{12,16},{16,20},{20,24},{24,28},{28,0},{1,5},{5... | collective-permute-start | bytes 49160 | tf_op jit(solution)/shard_map/ppermute | solution.py:26
  3.3 55.0 %collective-permute-start.1 = (f32[1,4,1,8,128]{4,3,2,1,0:T(8,128)}, f32[1,4,1,8,128]{4,3,2,1,0:T(8,128)}, u32[]{:S(2)}, u32[]{:S(2)}) collective-permute-start(f32[1,4,1,8,128]{4,3,2,1,0:T(8,128)} %get-tuple-element.39), channel_id=1, source_target_pairs={{0,28},{4,0},{8,4},{12,8},{16,12},{20,16},{24,20},{28,24},{1,29},{... | collective-permute-start | bytes 49160 | tf_op jit(solution)/shard_map/ppermute | solution.py:31
  18.0 6.4 %copy-start.13 = (s32[128]{0:T(128)}, s32[128]{0:T(128)S(1)}, u32[]{:S(2)}) copy-start(s32[128]{0:T(128)S(1)} %gather_fusion) | copy-start | bytes 1540
  43.5 35.0 %copy-start = (s32[1,128,128]{2,1,0:T(8,128)S(1)}, s32[1,128,128]{2,1,0:T(8,128)}, u32[]{:S(2)}) copy-start(s32[1,128,128]{2,1,0:T(8,128)} %param.16) | copy-start | bytes 196612
  43.6 35.0 %copy-start.1 = (f32[1,128,128]{2,1,0:T(8,128)S(1)}, f32[1,128,128]{2,1,0:T(8,128)}, u32[]{:S(2)}) copy-start(f32[1,128,128]{2,1,0:T(8,128)} %param.17) | copy-start | bytes 196612
  46.3 74.6 %copy-start.3 = (f32[1,8,128,128]{3,2,1,0:T(8,128)S(1)}, f32[1,8,128,128]{3,2,1,0:T(8,128)}, u32[]{:S(2)}) copy-start(f32[1,8,128,128]{3,2,1,0:T(8,128)} %param.14) | copy-start | bytes 1572868
  46.6 0.6 copy-start.8
  50.0 28.5 %copy-start.5 = (f32[1,1,8,128,128]{4,2,3,1,0:T(8,128)S(1)}, f32[1,1,8,128,128]{4,2,3,1,0:T(8,128)}, u32[]{:S(2)}) copy-start(f32[1,1,8,128,128]{4,2,3,1,0:T(8,128)} %maximum_add_fusion.1) | copy-start | bytes 1572868
  53.5 25.0 %copy-start.6 = (s32[128,128]{1,0:T(8,128)S(1)}, s32[128,128]{1,0:T(8,128)}, u32[]{:S(2)}) copy-start(s32[128,128]{1,0:T(8,128)} %broadcast_add_fusion) | copy-start | bytes 196612
  57.9 6.2 %collective-permute-start.2 = (f32[1,4,1,8,128]{4,3,2,1,0:T(8,128)}, f32[1,4,1,8,128]{4,3,2,1,0:T(8,128)S(1)}, u32[]{:S(2)}, u32[]{:S(2)}) collective-permute-start(f32[1,4,1,8,128]{4,3,2,1,0:T(8,128)} %collective-permute-done), channel_id=1, source_target_pairs={{0,4},{4,8},{8,12},{12,16},{16,20},{20,24},{24,28},{28,0},{1,5},{5... | collective-permute-start | bytes 49160 | tf_op jit(solution)/shard_map/ppermute | solution.py:26
  58.3 5.8 %collective-permute-start.3 = (f32[1,4,1,8,128]{4,3,2,1,0:T(8,128)}, f32[1,4,1,8,128]{4,3,2,1,0:T(8,128)S(1)}, u32[]{:S(2)}, u32[]{:S(2)}) collective-permute-start(f32[1,4,1,8,128]{4,3,2,1,0:T(8,128)} %collective-permute-done.1), channel_id=1, source_target_pairs={{0,28},{4,0},{8,4},{12,8},{16,12},{20,16},{24,20},{28,24},{1,29},{... | collective-permute-start | bytes 49160 | tf_op jit(solution)/shard_map/ppermute | solution.py:31
  64.1 5.0 %collective-permute-start.4 = (f32[1,4,1,8,128]{4,3,2,1,0:T(8,128)S(1)}, f32[1,4,1,8,128]{4,3,2,1,0:T(8,128)S(1)}, u32[]{:S(2)}, u32[]{:S(2)}) collective-permute-start(f32[1,4,1,8,128]{4,3,2,1,0:T(8,128)S(1)} %collective-permute-done.2), channel_id=1, source_target_pairs={{0,4},{4,8},{8,12},{12,16},{16,20},{20,24},{24,28},{28,0},{1,5},{5... | collective-permute-start | bytes 49160 | tf_op jit(solution)/shard_map/ppermute | solution.py:26
  64.1 5.6 %collective-permute-start.5 = (f32[1,4,1,8,128]{4,3,2,1,0:T(8,128)S(1)}, f32[1,4,1,8,128]{4,3,2,1,0:T(8,128)S(1)}, u32[]{:S(2)}, u32[]{:S(2)}) collective-permute-start(f32[1,4,1,8,128]{4,3,2,1,0:T(8,128)S(1)} %collective-permute-done.3), channel_id=1, source_target_pairs={{0,28},{4,0},{8,4},{12,8},{16,12},{20,16},{24,20},{28,24},{1,29},{... | collective-permute-start | bytes 49160 | tf_op jit(solution)/shard_map/ppermute | solution.py:31
  69.1 5.0 %collective-permute-start.6 = (f32[1,4,1,8,128]{4,3,2,1,0:T(8,128)S(1)}, f32[1,4,1,8,128]{4,3,2,1,0:T(8,128)S(1)}, u32[]{:S(2)}, u32[]{:S(2)}) collective-permute-start(f32[1,4,1,8,128]{4,3,2,1,0:T(8,128)S(1)} %collective-permute-done.4), channel_id=1, source_target_pairs={{0,4},{4,8},{8,12},{12,16},{16,20},{20,24},{24,28},{28,0},{1,5},{5... | collective-permute-start | bytes 49160 | tf_op jit(solution)/shard_map/ppermute | solution.py:26
  75.9 45.0 %copy-start.14 = (pred[8]{0:T(512)(128)(4,1)S(1)}, pred[8]{0:T(512)(128)(4,1)}, u32[]{:S(2)}) copy-start(pred[8]{0:T(512)(128)(4,1)} %iota_compare_fusion.11) | copy-start | bytes 28
  78.5 53.0 %copy-start.9 = (f32[128]{0:T(128)S(1)}, f32[128]{0:T(128)}, u32[]{:S(2)}) copy-start(f32[128]{0:T(128)} %gather_fusion.1) | copy-start | bytes 1540
  78.6 53.0 %copy-start.10 = (f32[128]{0:T(128)S(1)}, f32[128]{0:T(128)}, u32[]{:S(2)}) copy-start(f32[128]{0:T(128)} %get-tuple-element.9) | copy-start | bytes 1540
  78.6 53.0 %copy-start.11 = (f32[128]{0:T(128)S(1)}, f32[128]{0:T(128)}, u32[]{:S(2)}) copy-start(f32[128]{0:T(128)} %get-tuple-element.10) | copy-start | bytes 1540
  78.6 53.0 %copy-start.12 = (s32[128]{0:T(128)S(1)}, s32[128]{0:T(128)}, u32[]{:S(2)}) copy-start(s32[128]{0:T(128)} %broadcast_add_fusion.1) | copy-start | bytes 1540
